TPU v7x, 32 devices: a whole 2x2x4 slice. The times are simulated.
32 devices in a mesh: grp: 4 (over y, x), lm: 8 (over z, core).
Axes of the slice: x: 2, y: 2, z: 4, core: 2. Of those that a mesh axis runs over, the one named last changes fastest.
Arguments:
- embeddings: bfloat16 [8192, 512], P(('grp', 'lm')), may hold values from -14 to 14
- landmarks: bfloat16 [16384, 512], P('lm'), may hold values from -14 to 14
- start_vectors: float32 [8192, 128], P(('grp', 'lm')), may hold values from -10 to 10
- row_weight: float32 [8192], P(('grp', 'lm')), may hold values from 0.1 to 9
- spread: float32 [1], replicated, may hold values from 11.313708 to 33.941124
Outputs:
- subspace: float32 [8192, 128], P(('grp', 'lm'))
All inputs are finite; a program needn't handle non-finite values.
Results may differ from a plain program's by a relative error of at most 0.019.
Values may be sent and summed in bfloat16 or wider, within the bound.
A program may use at most 128 MiB of HBM per device.

v0:
```python
import jax
import jax.numpy as jnp
from jax import lax
from jax.sharding import PartitionSpec as P

ITERS = 2


def unit_rows(values):
    values = values.astype(jnp.float32)
    scale = lax.rsqrt(jnp.sum(values * values, axis=1, keepdims=True) + 1e-06)
    return (values * scale).astype(jnp.bfloat16)


def kernel_values(rows_unit, marks_unit, gamma):
    cosine = jnp.einsum("rd,ld->rl", rows_unit, marks_unit, preferred_element_type=jnp.float32)
    return jnp.exp(gamma * cosine)


def local(embeddings, landmarks, start_vectors, row_weight, spread):
    own_rows = embeddings.shape[0]
    marks = landmarks.shape[0]
    groups = lax.axis_size("grp")
    members = lax.axis_size("lm")
    total_rows = own_rows * groups * members
    group_rows = own_rows * members
    gamma = spread[0]
    rows_unit = unit_rows(embeddings)
    marks_unit = unit_rows(landmarks)
    sums = jnp.zeros((marks,), jnp.float32)
    weights = jnp.zeros((group_rows,), jnp.float32)
    part_rows = lax.all_gather(rows_unit, "lm", axis=0, tiled=True)
    part_weight = lax.all_gather(row_weight.astype(jnp.bfloat16), "lm", axis=0, tiled=True).astype(
        jnp.float32
    )
    values = kernel_values(part_rows, marks_unit, gamma)
    build_tile = values.astype(jnp.bfloat16)
    weights = lax.dynamic_update_slice_in_dim(weights, part_weight, jnp.int32(0), 0)
    sums = sums + jnp.sum(part_weight[:, None] * values, axis=0)
    mean_sum, weight_sum = lax.psum((sums, jnp.sum(weights)), "grp")
    means = mean_sum / weight_sum
    vectors = start_vectors
    weighted_full = row_weight[:, None] * vectors
    totals = lax.psum(jnp.sum(weighted_full, axis=0), ("grp", "lm"))
    group_weighted = lax.all_gather(weighted_full.astype(jnp.bfloat16), "lm", axis=0, tiled=True)
    for step in range(ITERS):
        side = (
            lax.psum(
                jnp.einsum(
                    "rl,rv->lv", build_tile, group_weighted, preferred_element_type=jnp.float32
                ),
                "grp",
            )
            - means[:, None] * totals[None, :]
        )
        side_b = side.astype(jnp.bfloat16)
        shift = jnp.dot(means, side_b.astype(jnp.float32), precision=lax.Precision.HIGHEST)
        partial_rows = weights[:, None] * (
            jnp.dot(build_tile, side_b, preferred_element_type=jnp.float32) - shift[None, :]
        )
        image = lax.psum(partial_rows, "lm")
        square, column = lax.psum(
            (jnp.sum(image * image, axis=0), jnp.sum(weights[:, None] * image, axis=0)), "grp"
        )
        scale = jnp.sqrt(square / total_rows + 1e-06)
        group_vectors = image / scale[None, :]
        totals = column / scale
        group_weighted = (weights[:, None] * group_vectors).astype(jnp.bfloat16)
        vectors = lax.dynamic_slice_in_dim(
            group_vectors, lax.axis_index("lm") * own_rows, own_rows, 0
        )
    return vectors


def solution(mesh):
    in_specs = (
        P(("grp", "lm"), None),
        P("lm", None),
        P(("grp", "lm"), None),
        P(("grp", "lm")),
        P(),
    )
    out_specs = P(("grp", "lm"), None)
    return jax.shard_map(local, mesh=mesh, in_specs=in_specs, out_specs=out_specs, check_vma=False)
```

profile of v0, /device:TPU:0, one launch (start us, length us, event | category | flops | bytes accessed | tf_op | source)
XLA Modules:
  0.0 337.8 jit_solution(3544346859675565320)
XLA Ops:
  6.5 0.0 all-gather.3.cloned.1.call-start
  6.5 1.1 fusion.8
  7.6 1.8 fusion.9
  9.4 0.0 all-gather.3.cloned.1.call-update
  9.4 0.0 all-reduce.7.cloned.1.call-start
  9.5 0.7 convert_element_type.35
  10.2 13.5 %all-gather = bf16[8,1,256]{2,1,0:T(2,128)(2,1)S(1)} all-gather(bf16[1,1,256]{2,1,0:T(2,128)(2,1)S(1)} %reshape.21), channel_id=1, replica_groups=mesh['grp'=4,'lm'=8] {'lm'}, dimensions={0}, use_global_device_ids=true | all-gather | bytes 4608 | tf_op jit(solution)/shard_map/all_gather | solution.py:33
  24.3 2.1 fusion.1
  26.4 1.0 multiply_reduce_fusion.4
  27.4 17.3 %all_gather.11 = bf16[2048,128]{1,0:T(8,128)(2,1)S(1)} all-gather(bf16[256,128]{1,0:T(8,128)(2,1)S(1)} %get-tuple-element.14), channel_id=1, replica_groups=mesh['grp'=4,'lm'=8] {'lm'}, dimensions={0}, use_global_device_ids=true | all-gather | bytes 589824 | tf_op jit(solution)/shard_map/all_gather | solution.py:45
  44.7 1.0 all-gather.3.cloned.1.call-done
  45.7 7.8 %multiply_reduce_fusion = (f32[2048]{0:T(1024)S(1)}, bf16[2048,2048]{1,0:T(8,128)(2,1)S(1)}) fusion(f32[2048]{0:T(1024)S(1)} %bitcast.19, f32[]{:T(128)} %bitcast.16, bf16[2048,512]{1,0:T(8,128)(2,1)} %all-gather.3.cloned.1.call-done, bf16[2048,512]{1,0:T(8,128)(2,1)} %param.6, f32[2048]{0:T(1024)S(1)} %add_rsqrt_fusion), kind=kOutput, calls=%fused_computation | convolution fusion | flops 4314888192 | bytes 12607492 | tf_op jit(solution)/shard_map/rd,ld->rl/dot_general | solution.py:16
  53.5 0.0 copy-start
  53.5 3.2 copy-done
  56.7 3.4 %fusion.14 = f32[2048,128]{1,0:T(8,128)} fusion(bf16[2048,2048]{1,0:T(8,128)(2,1)S(1)} %get-tuple-element.12, bf16[2048,128]{1,0:T(8,128)(2,1)S(1)} %all_gather.11), kind=kOutput, calls=%fused_computation.38 | convolution fusion | flops 1073741824 | bytes 9961472 | tf_op jit(solution)/shard_map/rl,rv->lv/dot_general | solution.py:49
  60.2 0.0 all-reduce.7.cloned.1.call-update
  60.2 0.0 all-reduce.9.cloned.1.call-start
  60.2 40.3 %psum.73 = f32[128]{0:T(128)S(1)} all-reduce(f32[128]{0:T(128)S(1)} %get-tuple-element.13), channel_id=1, replica_groups=mesh['grp'=4,'lm'=8] {'grp','lm'}, use_global_device_ids=true, to_apply=%region_8.0 | all-reduce | flops 128 | bytes 1024 | tf_op jit(solution)/shard_map/psum | solution.py:44
  100.5 0.6 convert_reduce_fusion
  101.1 11.7 %all-reduce.1 = (f32[2048]{0:T(1024)S(1)}, f32[]{:T(128)}) all-reduce(f32[2048]{0:T(1024)S(1)} %get-tuple-element.11, f32[]{:T(128)} %convert_reduce_fusion), channel_id=1, replica_groups=mesh['grp'=4,'lm'=8] {'grp'}, use_global_device_ids=true, to_apply=%region_4.0 | all-reduce | flops 2049 | bytes 16392 | tf_op jit(solution)/shard_map/psum | solution.py:40
  112.8 0.6 broadcast_divide_fusion
  113.5 0.0 all-reduce.7.cloned.1.call-done
  113.5 1.8 convolution_bitcast_fusion.1
  115.3 7.1 %fusion.4 = f32[2048,128]{1,0:T(8,128)} fusion(bf16[2048,2048]{1,0:T(8,128)(2,1)} %copy-done, f32[128]{0:T(128)S(1)} %convolution_bitcast_fusion.1, f32[2048]{0:T(1024)S(1)} %bitcast.20, f32[2048,128]{1,0:T(8,128)} %all-reduce.7.cloned.1.call-done, f32[128]{0:T(128)S(1)} %psum.73, f32[2048]{0:T(1024)S(1)} %broadcast_divide_fusion), kind=kOutput, calls=%fused_computation.10 | convolution fusion | flops 1075052544 | bytes 10503168 | tf_op jit(solution)/shard_map/dot_general | solution.py:59
  122.4 0.0 all-reduce.9.cloned.1.call-update
  122.4 0.0 all-reduce.11.cloned.1.call-start
  122.5 58.7 %all-reduce.9.cloned.1.call-done = f32[2048,128]{1,0:T(8,128)} async-done(((f32[2048,128]{1,0:T(8,128)}), f32[2048,128]{1,0:T(8,128)}) %all-reduce.9.cloned.1.call-update) | async-done | bytes 1048592 | tf_op jit(solution)/shard_map/psum | solution.py:61
  181.1 1.6 multiply_reduce_fusion.2
  182.7 10.0 %all-reduce = (f32[128]{0:T(128)S(1)}, f32[128]{0:T(128)S(1)}) all-reduce(f32[128]{0:T(128)S(1)} %get-tuple-element.6, f32[128]{0:T(128)S(1)} %get-tuple-element.5), channel_id=1, replica_groups=mesh['grp'=4,'lm'=8] {'grp'}, use_global_device_ids=true, to_apply=%region_11.0 | all-reduce | flops 256 | bytes 2048 | tf_op jit(solution)/shard_map/psum | solution.py:62
  192.7 7.3 %fusion.10 = f32[2048,128]{1,0:T(8,128)} fusion(bf16[2048,2048]{1,0:T(8,128)(2,1)} %copy-done, f32[2048,128]{1,0:T(8,128)} %all-reduce.9.cloned.1.call-done, f32[128]{0:T(128)S(1)} %get-tuple-element.16, f32[2048]{0:T(1024)S(1)} %bitcast.22), kind=kOutput, calls=%fused_computation.25 | convolution fusion | flops 1074528256 | bytes 10494464 | tf_op jit(solution)/shard_map/rl,rv->lv/dot_general | solution.py:49
  200.0 0.0 all-reduce.11.cloned.1.call-update
  200.0 0.0 all-reduce.13.cloned.1.call-start
  200.1 49.9 %all-reduce.11.cloned.1.call-done = f32[2048,128]{1,0:T(8,128)} async-done(((f32[2048,128]{1,0:T(8,128)}), f32[2048,128]{1,0:T(8,128)}) %all-reduce.11.cloned.1.call-update) | async-done | bytes 1048592 | tf_op jit(solution)/shard_map/psum | solution.py:48
  250.0 1.8 convolution_bitcast_fusion
  251.8 7.1 %fusion.3 = f32[2048,128]{1,0:T(8,128)} fusion(bf16[2048,2048]{1,0:T(8,128)(2,1)} %copy-done, f32[128]{0:T(128)S(1)} %convolution_bitcast_fusion, f32[2048]{0:T(1024)S(1)} %bitcast.23, f32[2048,128]{1,0:T(8,128)} %all-reduce.11.cloned.1.call-done, f32[128]{0:T(128)S(1)} %get-tuple-element.15, f32[2048]{0:T(1024)S(1)} %broadcast_divide_fusion), kind=kOutput, calls=%fused_computation.8 | convolution fusion | flops 1075052544 | bytes 10503168 | tf_op jit(solution)/shard_map/dot_general | solution.py:59
  258.9 0.0 all-reduce.13.cloned.1.call-update
  258.9 59.5 %all-reduce.13.cloned.1.call-done = f32[2048,128]{1,0:T(8,128)} async-done(((f32[2048,128]{1,0:T(8,128)}), f32[2048,128]{1,0:T(8,128)}) %all-reduce.13.cloned.1.call-update) | async-done | bytes 1048592 | tf_op jit(solution)/shard_map/psum | solution.py:61
  318.4 1.5 multiply_reduce_fusion.1
  319.9 9.8 %psum.79 = f32[128]{0:T(128)S(1)} all-reduce(f32[128]{0:T(128)S(1)} %multiply_reduce_fusion.1), channel_id=1, replica_groups=mesh['grp'=4,'lm'=8] {'grp'}, use_global_device_ids=true, to_apply=%region_17.0 | all-reduce | flops 128 | bytes 1024 | tf_op jit(solution)/shard_map/psum | solution.py:62
  329.7 1.6 dynamic-slice_divide_fusion
  (6 shorter events, 0.1 us)
Async XLA Ops:
  6.5 39.1 %all-gather.3.cloned.1.call-start = ((), (), s32[]{:S(2)}) async-start(), calls=%async_computation | async-start | bytes 2359296 | tf_op jit(solution)/shard_map/all_gather | solution.py:32
  9.4 104.1 %all-reduce.7.cloned.1.call-start = ((), (), s32[]{:S(2)}) async-start(), calls=%async_computation.1 | async-start | bytes 2097152 | tf_op jit(solution)/shard_map/psum | solution.py:48
  53.5 3.2 copy-start
  60.2 120.9 %all-reduce.9.cloned.1.call-start = ((), (), s32[]{:S(2)}) async-start(), calls=%async_computation.2 | async-start | bytes 2097152 | tf_op jit(solution)/shard_map/psum | solution.py:61
  122.4 127.6 %all-reduce.11.cloned.1.call-start = ((), (), s32[]{:S(2)}) async-start(), calls=%async_computation.3 | async-start | bytes 2097152 | tf_op jit(solution)/shard_map/psum | solution.py:48
  200.0 118.3 %all-reduce.13.cloned.1.call-start = ((), (), s32[]{:S(2)}) async-start(), calls=%async_computation.4 | async-start | bytes 2097152 | tf_op jit(solution)/shard_map/psum | solution.py:61
Sparse Core Ops, SparseCore 0:
  9.6 36.0 all-gather.2
  60.3 52.8 all-reduce.6
  122.5 58.5 all-reduce.8
  200.2 49.8 all-reduce.10
  259.0 59.2 all-reduce.12
where the time goes:
time: 338 us
  waiting for transfers between devices  169 us (50%)
  blocking collectives  102 us (30%)
  matrix products  36.3 us (11%)
  between operations  13.9 us (4%)
  other arithmetic  12.6 us (4%)
    psum x2, waiting for transfers between devices, local(): image = lax.psum(partial_rows, 'lm')  118 us
    psum x2, waiting for transfers between devices, local(): lax.psum(jnp.einsum('rl,rv->lv', build_tile, group_weighted, preferred_el...  50 us
    psum x1, blocking collectives, local(): totals = lax.psum(jnp.sum(weighted_full, axis=0), ('grp', 'lm'))  40.3 us
    psum x2, blocking collectives, local(): lax.psum((jnp.sum(image * image, axis=0), jnp.sum(weights[:, None] * imag...  19.7 us
    all_gather x1, blocking collectives, local(): lax.all_gather(weighted_full.astype(jnp.bfloat16), 'lm', axis=0, tiled=True)  17.3 us
    dot_general x2, matrix products, local(): jnp.dot(build_tile, side_b, preferred_element_type=jnp.float32)  14.1 us
    all_gather x1, blocking collectives, local(): lax.all_gather(row_weight.astype(jnp.bfloat16), 'lm', axis=0, tiled=True)  13.5 us
    psum x1, blocking collectives, local(): mean_sum, weight_sum = lax.psum((sums, jnp.sum(weights)), 'grp')  11.7 us
  transfers between devices with their start and end apart: 5, of which 4 were waited for; matrix products, arithmetic and copies ran while one was open for 1% of the time, Pallas kernels for 0%

commit v1 on v0

--- a/solution.py
+++ b/solution.py
@@ -58,7 +58,9 @@
         partial_rows = weights[:, None] * (
             jnp.dot(build_tile, side_b, preferred_element_type=jnp.float32) - shift[None, :]
         )
-        image = lax.psum(partial_rows, "lm")
+        image = partial_rows
+        for hop in (1, 2, 4):
+            image = image + lax.ppermute(image, "lm", [(dev, dev ^ hop) for dev in range(8)])
         square, column = lax.psum(
             (jnp.sum(image * image, axis=0), jnp.sum(weights[:, None] * image, axis=0)), "grp"
         )

time: 338 us -> 367 us (1.086)
  waiting for transfers between devices: 169 us -> 198 us
  starting transfers between devices: 0.17 us -> 7.26 us
    ppermute x0 -> x6, waiting for transfers between devices: none -> 144 us  [local(): lax.ppermute(image, 'lm', [(dev, dev ^ hop) for dev in range(8)])]
    psum x2 -> x0, waiting for transfers between devices: 118 us -> none  [local(): image = lax.psum(partial_rows, 'lm')]
    ppermute x0 -> x6, starting transfers between devices: none -> 7.18 us  [local(): lax.ppermute(image, 'lm', [(dev, dev ^ hop) for dev in range(8)])]
  transfers between devices with their start and end apart: 5 -> 9, of which waited for: 4 -> 8; matrix products, arithmetic and copies ran while one was open for 1% -> 1% of each run, Pallas kernels for 0% -> 0%
where the time goes in v1:
time: 367 us; the launch traced here: 366 us
  waiting for transfers between devices  198 us (54%)
  blocking collectives  100 us (27%)
  matrix products  34.1 us (9%)
  between operations  13.9 us (4%)
  other arithmetic  9.71 us (3%)
  starting transfers between devices  7.26 us (2%)
    ppermute x6, waiting for transfers between devices, local(): lax.ppermute(image, 'lm', [(dev, dev ^ hop) for dev in range(8)])  144 us
    psum x2, waiting for transfers between devices, local(): lax.psum(jnp.einsum('rl,rv->lv', build_tile, group_weighted, preferred_el...  52.2 us
    psum x1, blocking collectives, local(): totals = lax.psum(jnp.sum(weighted_full, axis=0), ('grp', 'lm'))  40.3 us
    psum x2, blocking collectives, local(): lax.psum((jnp.sum(image * image, axis=0), jnp.sum(weights[:, None] * imag...  17.7 us
    all_gather x1, blocking collectives, local(): lax.all_gather(weighted_full.astype(jnp.bfloat16), 'lm', axis=0, tiled=True)  17.3 us
    all_gather x1, blocking collectives, local(): lax.all_gather(row_weight.astype(jnp.bfloat16), 'lm', axis=0, tiled=True)  13.5 us
    dot_general x2, matrix products, local(): jnp.dot(build_tile, side_b, preferred_element_type=jnp.float32)  12.2 us
    psum x1, blocking collectives, local(): mean_sum, weight_sum = lax.psum((sums, jnp.sum(weights)), 'grp')  11.7 us
  transfers between devices with their start and end apart: 9, of which 8 were waited for; matrix products, arithmetic and copies ran while one was open for 1% of the time, Pallas kernels for 0%

profile of v1, /device:TPU:0, one launch (start us, length us, event | category | flops | bytes accessed | tf_op | source)
XLA Modules:
  0.0 366.2 jit_solution(5030852468052424257)
XLA Ops:
  6.5 0.0 all-gather.3.cloned.1.call-start
  6.5 1.1 fusion.8
  7.6 1.8 fusion.9
  9.4 0.0 all-gather.3.cloned.1.call-update
  9.4 0.0 all-reduce.5.cloned.1.call-start
  9.5 0.7 convert_element_type.35
  10.2 13.5 %all-gather = bf16[8,1,256]{2,1,0:T(2,128)(2,1)S(1)} all-gather(bf16[1,1,256]{2,1,0:T(2,128)(2,1)S(1)} %reshape.21), channel_id=1, replica_groups=mesh['grp'=4,'lm'=8] {'lm'}, dimensions={0}, use_global_device_ids=true | all-gather | bytes 4608 | tf_op jit(solution)/shard_map/all_gather | solution.py:33
  24.3 2.1 fusion.1
  26.4 1.0 multiply_reduce_fusion.4
  27.4 17.3 %all_gather.11 = bf16[2048,128]{1,0:T(8,128)(2,1)S(1)} all-gather(bf16[256,128]{1,0:T(8,128)(2,1)S(1)} %get-tuple-element.17), channel_id=1, replica_groups=mesh['grp'=4,'lm'=8] {'lm'}, dimensions={0}, use_global_device_ids=true | all-gather | bytes 589824 | tf_op jit(solution)/shard_map/all_gather | solution.py:45
  44.7 1.0 all-gather.3.cloned.1.call-done
  45.7 7.8 %multiply_reduce_fusion = (f32[2048]{0:T(1024)S(1)}, bf16[2048,2048]{1,0:T(8,128)(2,1)S(1)}) fusion(f32[2048]{0:T(1024)S(1)} %bitcast.19, f32[]{:T(128)} %bitcast.16, bf16[2048,512]{1,0:T(8,128)(2,1)} %all-gather.3.cloned.1.call-done, bf16[2048,512]{1,0:T(8,128)(2,1)} %param.6, f32[2048]{0:T(1024)S(1)} %add_rsqrt_fusion), kind=kOutput, calls=%fused_computation | convolution fusion | flops 4314888192 | bytes 12607492 | tf_op jit(solution)/shard_map/rd,ld->rl/dot_general | solution.py:16
  53.5 0.0 copy-start
  53.5 3.2 copy-done
  56.7 3.4 fusion.14
  60.1 0.0 all-reduce.5.cloned.1.call-update
  60.1 0.0 all-reduce.7.cloned.1.call-start
  60.2 40.3 %psum.59 = f32[128]{0:T(128)S(1)} all-reduce(f32[128]{0:T(128)S(1)} %get-tuple-element.16), channel_id=1, replica_groups=mesh['grp'=4,'lm'=8] {'grp','lm'}, use_global_device_ids=true, to_apply=%region_8.0 | all-reduce | flops 128 | bytes 1024 | tf_op jit(solution)/shard_map/psum | solution.py:44
  100.4 0.6 convert_reduce_fusion
  101.0 11.7 %all-reduce.1 = (f32[2048]{0:T(1024)S(1)}, f32[]{:T(128)}) all-reduce(f32[2048]{0:T(1024)S(1)} %get-tuple-element.14, f32[]{:T(128)} %convert_reduce_fusion), channel_id=1, replica_groups=mesh['grp'=4,'lm'=8] {'grp'}, use_global_device_ids=true, to_apply=%region_4.0 | all-reduce | flops 2049 | bytes 16392 | tf_op jit(solution)/shard_map/psum | solution.py:40
  112.8 0.6 broadcast_divide_fusion
  113.4 0.0 all-reduce.5.cloned.1.call-done
  113.5 1.8 convolution_bitcast_fusion.1
  115.3 6.1 %fusion.4 = f32[2048,128]{1,0:T(8,128)S(1)} fusion(bf16[2048,2048]{1,0:T(8,128)(2,1)} %copy-done, f32[128]{0:T(128)S(1)} %convolution_bitcast_fusion.1, f32[2048]{0:T(1024)S(1)} %bitcast.20, f32[2048,128]{1,0:T(8,128)} %all-reduce.5.cloned.1.call-done, f32[128]{0:T(128)S(1)} %psum.59, f32[2048]{0:T(1024)S(1)} %broadcast_divide_fusion), kind=kOutput, calls=%fused_computation.10 | convolution fusion | flops 1075052544 | bytes 10503168 | tf_op jit(solution)/shard_map/dot_general | solution.py:59
  121.4 0.1 collective-permute-start
  121.5 2.6 collective-permute-done
  124.1 0.1 add.69
  124.2 1.2 collective-permute-start.1
  125.4 24.1 %collective-permute-done.1 = f32[2048,128]{1,0:T(8,128)S(1)} collective-permute-done((f32[2048,128]{1,0:T(8,128)S(1)}, f32[2048,128]{1,0:T(8,128)S(1)}, u32[]{:S(2)}, u32[]{:S(2)}) %collective-permute-start.1) | collective-permute-done | bytes 1048608 | tf_op jit(solution)/shard_map/ppermute | solution.py:63
  149.5 0.1 add.70
  149.6 1.8 collective-permute-start.2
  151.4 45.9 %collective-permute-done.2 = f32[2048,128]{1,0:T(8,128)S(1)} collective-permute-done((f32[2048,128]{1,0:T(8,128)S(1)}, f32[2048,128]{1,0:T(8,128)S(1)}, u32[]{:S(2)}, u32[]{:S(2)}) %collective-permute-start.2) | collective-permute-done | bytes 1048608 | tf_op jit(solution)/shard_map/ppermute | solution.py:63
  197.4 0.4 multiply_reduce_fusion.2
  197.7 8.8 %all-reduce = (f32[128]{0:T(128)S(1)}, f32[128]{0:T(128)S(1)}) all-reduce(f32[128]{0:T(128)S(1)} %get-tuple-element.6, f32[128]{0:T(128)S(1)} %get-tuple-element.5), channel_id=1, replica_groups=mesh['grp'=4,'lm'=8] {'grp'}, use_global_device_ids=true, to_apply=%region_10.0 | all-reduce | flops 256 | bytes 2048 | tf_op jit(solution)/shard_map/psum | solution.py:64
  206.5 7.1 %fusion.10 = f32[2048,128]{1,0:T(8,128)} fusion(bf16[2048,2048]{1,0:T(8,128)(2,1)} %copy-done, f32[2048,128]{1,0:T(8,128)S(1)} %get-tuple-element.13, f32[128]{0:T(128)S(1)} %get-tuple-element.19, f32[2048]{0:T(1024)S(1)} %bitcast.22), kind=kOutput, calls=%fused_computation.25 | convolution fusion | flops 1074528256 | bytes 10494464 | tf_op jit(solution)/shard_map/rl,rv->lv/dot_general | solution.py:49
  213.7 0.0 all-reduce.7.cloned.1.call-update
  213.7 52.2 %all-reduce.7.cloned.1.call-done = f32[2048,128]{1,0:T(8,128)} async-done(((f32[2048,128]{1,0:T(8,128)}), f32[2048,128]{1,0:T(8,128)}) %all-reduce.7.cloned.1.call-update) | async-done | bytes 1048592 | tf_op jit(solution)/shard_map/psum | solution.py:48
  265.9 1.8 convolution_bitcast_fusion
  267.7 6.1 %fusion.3 = f32[2048,128]{1,0:T(8,128)S(1)} fusion(bf16[2048,2048]{1,0:T(8,128)(2,1)} %copy-done, f32[128]{0:T(128)S(1)} %convolution_bitcast_fusion, f32[2048]{0:T(1024)S(1)} %bitcast.23, f32[2048,128]{1,0:T(8,128)} %all-reduce.7.cloned.1.call-done, f32[128]{0:T(128)S(1)} %get-tuple-element.18, f32[2048]{0:T(1024)S(1)} %broadcast_divide_fusion), kind=kOutput, calls=%fused_computation.8 | convolution fusion | flops 1075052544 | bytes 10503168 | tf_op jit(solution)/shard_map/dot_general | solution.py:59
  273.8 0.1 collective-permute-start.3
  273.9 2.6 collective-permute-done.3
  276.5 0.1 add.73
  276.6 1.6 collective-permute-start.4
  278.2 23.7 %collective-permute-done.4 = f32[2048,128]{1,0:T(8,128)S(1)} collective-permute-done((f32[2048,128]{1,0:T(8,128)S(1)}, f32[2048,128]{1,0:T(8,128)S(1)}, u32[]{:S(2)}, u32[]{:S(2)}) %collective-permute-start.4) | collective-permute-done | bytes 1048608 | tf_op jit(solution)/shard_map/ppermute | solution.py:63
  301.9 0.1 add.74
  302.0 2.5 collective-permute-start.5
  304.5 45.3 %collective-permute-done.5 = f32[2048,128]{1,0:T(8,128)S(1)} collective-permute-done((f32[2048,128]{1,0:T(8,128)S(1)}, f32[2048,128]{1,0:T(8,128)S(1)}, u32[]{:S(2)}, u32[]{:S(2)}) %collective-permute-start.5) | collective-permute-done | bytes 1048608 | tf_op jit(solution)/shard_map/ppermute | solution.py:63
  349.8 0.3 multiply_reduce_fusion.1
  350.1 8.9 %psum.63 = f32[128]{0:T(128)S(1)} all-reduce(f32[128]{0:T(128)S(1)} %get-tuple-element.11), channel_id=1, replica_groups=mesh['grp'=4,'lm'=8] {'grp'}, use_global_device_ids=true, to_apply=%region_15.0 | all-reduce | flops 128 | bytes 1024 | tf_op jit(solution)/shard_map/psum | solution.py:64
  359.0 0.7 dynamic-slice_divide_fusion
  (6 shorter events, 0.1 us)
Async XLA Ops:
  6.5 39.1 %all-gather.3.cloned.1.call-start = ((), (), s32[]{:S(2)}) async-start(), calls=%async_computation | async-start | bytes 2359296 | tf_op jit(solution)/shard_map/all_gather | solution.py:32
  9.4 104.0 %all-reduce.5.cloned.1.call-start = ((), (), s32[]{:S(2)}) async-start(), calls=%async_computation.1 | async-start | bytes 2097152 | tf_op jit(solution)/shard_map/psum | solution.py:48
  53.5 3.2 copy-start
  60.1 205.7 %all-reduce.7.cloned.1.call-start = ((), (), s32[]{:S(2)}) async-start(), calls=%async_computation.2 | async-start | bytes 2097152 | tf_op jit(solution)/shard_map/psum | solution.py:48
  121.4 2.7 collective-permute-start
  124.2 25.3 %collective-permute-start.1 = (f32[2048,128]{1,0:T(8,128)S(1)}, f32[2048,128]{1,0:T(8,128)S(1)}, u32[]{:S(2)}, u32[]{:S(2)}) collective-permute-start(f32[2048,128]{1,0:T(8,128)S(1)} %add.69), channel_id=1, source_target_pairs={{0,2},{1,3},{2,0},{3,1},{4,6},{5,7},{6,4},{7,5},{8,10},{9,11},{10,... | collective-permute-start | bytes 3145736 | tf_op jit(solution)/shard_map/ppermute | solution.py:63
  149.6 47.8 %collective-permute-start.2 = (f32[2048,128]{1,0:T(8,128)S(1)}, f32[2048,128]{1,0:T(8,128)S(1)}, u32[]{:S(2)}, u32[]{:S(2)}) collective-permute-start(f32[2048,128]{1,0:T(8,128)S(1)} %add.70), channel_id=1, source_target_pairs={{0,4},{1,5},{2,6},{3,7},{4,0},{5,1},{6,2},{7,3},{8,12},{9,13},{10,... | collective-permute-start | bytes 3145736 | tf_op jit(solution)/shard_map/ppermute | solution.py:63
  273.8 2.7 collective-permute-start.3
  276.6 25.3 %collective-permute-start.4 = (f32[2048,128]{1,0:T(8,128)S(1)}, f32[2048,128]{1,0:T(8,128)S(1)}, u32[]{:S(2)}, u32[]{:S(2)}) collective-permute-start(f32[2048,128]{1,0:T(8,128)S(1)} %add.73), channel_id=1, source_target_pairs={{0,2},{1,3},{2,0},{3,1},{4,6},{5,7},{6,4},{7,5},{8,10},{9,11},{10,... | collective-permute-start | bytes 3145736 | tf_op jit(solution)/shard_map/ppermute | solution.py:63
  302.0 47.8 %collective-permute-start.5 = (f32[2048,128]{1,0:T(8,128)S(1)}, f32[2048,128]{1,0:T(8,128)S(1)}, u32[]{:S(2)}, u32[]{:S(2)}) collective-permute-start(f32[2048,128]{1,0:T(8,128)S(1)} %add.74), channel_id=1, source_target_pairs={{0,4},{1,5},{2,6},{3,7},{4,0},{5,1},{6,2},{7,3},{8,12},{9,13},{10,... | collective-permute-start | bytes 3145736 | tf_op jit(solution)/shard_map/ppermute | solution.py:63
Sparse Core Ops, SparseCore 0:
  9.6 36.0 all-gather.2
  60.2 52.8 all-reduce.4
  213.8 51.9 all-reduce.6
